TPU v7x, 32 devices: a whole 2x2x4 slice. The times are simulated.
32 devices in a mesh: fsdp: 16 (over z, x, core), dp: 2 (over y).
Axes of the slice: x: 2, y: 2, z: 4, core: 2. Of those that a mesh axis runs over, the one named last changes fastest.
Arguments:
- inputs: bfloat16 [6144, 4096], P(('fsdp', 'dp')), may hold values from -6 to 6
- grad_out: bfloat16 [6144, 14336], P(('fsdp', 'dp')), may hold values from -0.009765625 to 0.009765625
- projection: bfloat16 [4096, 128], P('fsdp'), may hold values from -0.375 to 0.375
- moment: float32 [14336, 128], P('fsdp'), may hold values from -1.5 to 1.5
- second: float32 [14336, 128], P('fsdp'), may hold values from 0.0001 to 0.001
Outputs:
- update: bfloat16 [4096, 14336], P('fsdp')
- new_moment: float32 [14336, 128], P('fsdp')
- new_second: float32 [14336, 128], P('fsdp')
All inputs are finite; a program needn't handle non-finite values.
Results may differ from a plain program's by a relative error of at most 0.0051.
Values may be sent and summed in bfloat16 or wider, within the bound.
No kernel may reach another device: no remote copies, remote signals or barrier semaphores. Data moves between devices by JAX's collectives and lax.ppermute only.
A program may use at most 64 MiB of HBM per device.

v0:
```python
import jax
import jax.numpy as jnp
from jax import lax
from jax.sharding import PartitionSpec as P

STEP = 10


def adam_step(low_rank, moment, second):
    new_moment = 0.9 * moment + 0.1 * low_rank
    new_second = 0.999 * second + 0.001 * (low_rank * low_rank)
    first_fix = 1.0 - 0.9**STEP
    second_fix = 1.0 - 0.999**STEP
    normalized = (new_moment / first_fix / (jnp.sqrt(new_second / second_fix) + 1e-08)).astype(
        jnp.bfloat16
    )
    return (new_moment, new_second, normalized)


def local(inputs, grad_out, projection, moment, second):
    projected = jnp.dot(
        inputs,
        lax.all_gather(projection, "fsdp", axis=0, tiled=True),
        preferred_element_type=jnp.float32,
    ).astype(jnp.bfloat16)
    contract = (((0,), (0,)), ((), ()))
    whole = lax.dot_general(grad_out, projected, contract, preferred_element_type=jnp.float32)
    whole = lax.psum(whole, "dp")
    low_rank = lax.psum_scatter(whole, "fsdp", scatter_dimension=0, tiled=True)
    new_moment, new_second, normalized = adam_step(low_rank, moment, second)
    expand = (((1,), (1,)), ((), ()))
    update = lax.dot_general(
        projection,
        lax.all_gather(normalized, "fsdp", axis=0, tiled=True),
        expand,
        preferred_element_type=jnp.float32,
    ).astype(jnp.bfloat16)
    return (update, new_moment, new_second)


def solution(mesh):
    in_specs = (
        P(("fsdp", "dp"), None),
        P(("fsdp", "dp"), None),
        P("fsdp", None),
        P("fsdp", None),
        P("fsdp", None),
    )
    out_specs = (P("fsdp", None), P("fsdp", None), P("fsdp", None))
    return jax.shard_map(local, mesh=mesh, in_specs=in_specs, out_specs=out_specs, check_vma=False)
```

profile of v0, /device:TPU:0, one launch (start us, length us, event | category | flops | bytes accessed | tf_op | source)
XLA Modules:
  0.0 252.6 jit_solution(8466995799311963233)
XLA Ops:
  7.2 0.0 copy-start
  7.2 0.0 all-gather.3.cloned.1.call-start
  7.2 0.7 all-gather.3.cloned.1.call-update
  7.9 0.0 reduce-scatter.2.cloned.1.call-start
  8.0 42.8 %all-gather.3.cloned.1.call-done = bf16[4096,128]{1,0:T(8,128)(2,1)} async-done(((bf16[256,128]{1,0:T(8,128)(2,1)}), bf16[4096,128]{1,0:T(8,128)(2,1)}) %all-gather.3.cloned.1.call-update) | async-done | bytes 1048592 | tf_op jit(solution)/shard_map/all_gather | solution.py:23
  50.7 0.0 copy-done
  50.7 7.6 %convolution_bitcast_fusion = f32[14336,128]{0,1:T(8,128)} fusion(bf16[192,14336]{1,0:T(8,128)(2,1)} %param.6, bf16[192,4096]{1,0:T(8,128)(2,1)S(1)} %copy-done, bf16[4096,128]{1,0:T(8,128)(2,1)} %all-gather.3.cloned.1.call-done), kind=kOutput, calls=%fused_computation.2 | convolution fusion | flops 905994240 | bytes 15466496 | tf_op jit(solution)/shard_map/dot_general | solution.py:27
  58.4 0.0 copy-start.1
  58.4 0.0 copy-start.2
  58.4 0.0 copy-start.3
  58.4 0.0 reduce-scatter.2.cloned.1.call-update
  58.4 0.0 all-reduce.2.cloned.1.call-start
  58.5 90.7 %reduce-scatter.2.cloned.1.call-done = f32[896,128]{0,1:T(8,128)} async-done(((f32[14336,128]{0,1:T(8,128)}), f32[896,128]{0,1:T(8,128)}) %reduce-scatter.2.cloned.1.call-update) | async-done | bytes 458768 | tf_op jit(solution)/shard_map/reduce_scatter | solution.py:29
  149.2 0.0 all-reduce.2.cloned.1.call-update
  149.2 0.0 all-gather.5.cloned.1.call-start
  149.3 0.0 copy-done.1
  149.3 0.2 copy.8
  149.5 0.0 copy-done.2
  149.5 0.2 copy.9
  149.7 28.8 %all-reduce.2.cloned.1.call-done = f32[896,128]{0,1:T(8,128)} async-done(((f32[896,128]{0,1:T(8,128)}), f32[896,128]{0,1:T(8,128)}) %all-reduce.2.cloned.1.call-update) | async-done | bytes 458768 | tf_op jit(solution)/shard_map/psum | solution.py:28
  178.5 2.0 divide_convert_fusion
  180.5 0.0 all-gather.5.cloned.1.call-update
  180.5 1.0 copy.11
  181.5 1.0 copy.12
  182.4 46.4 %all-gather.5.cloned.1.call-done = bf16[14336,128]{0,1:T(8,128)(2,1)} async-done(((bf16[896,128]{0,1:T(8,128)(2,1)}), bf16[14336,128]{0,1:T(8,128)(2,1)}) %all-gather.5.cloned.1.call-update) | async-done | bytes 3670032 | tf_op jit(solution)/shard_map/all_gather | solution.py:34
  228.9 0.0 copy-done.3
  228.9 7.1 %fusion = bf16[256,14336]{0,1:T(8,128)(2,1)} fusion(bf16[14336,128]{0,1:T(8,128)(2,1)} %all-gather.5.cloned.1.call-done, bf16[256,128]{1,0:T(8,128)(2,1)S(1)} %copy-done.3), kind=kOutput, calls=%fused_computation.1 | convolution fusion | flops 943194112 | bytes 11075584 | tf_op jit(solution)/shard_map/dot_general | solution.py:32
  236.0 10.1 %copy.10 = bf16[256,14336]{1,0:T(8,128)(2,1)} copy(bf16[256,14336]{0,1:T(8,128)(2,1)} %fusion) | data formatting | bytes 14680064
Async XLA Ops:
  7.2 43.6 %copy-start = (bf16[192,4096]{1,0:T(8,128)(2,1)S(1)}, bf16[192,4096]{1,0:T(8,128)(2,1)}, u32[]{:S(2)}) copy-start(bf16[192,4096]{1,0:T(8,128)(2,1)} %param.5) | copy-start | bytes 4718596
  7.2 43.6 %all-gather.3.cloned.1.call-start = ((), (), s32[]{:S(2)}) async-start(), calls=%async_computation.1 | async-start | bytes 1114112 | tf_op jit(solution)/shard_map/all_gather | solution.py:23
  7.9 141.3 %reduce-scatter.2.cloned.1.call-start = ((), (), s32[]{:S(2)}) async-start(), calls=%async_computation.3 | async-start | bytes 7798784 | tf_op jit(solution)/shard_map/reduce_scatter | solution.py:29
  58.4 90.9 %copy-start.1 = (f32[896,128]{1,0:T(8,128)S(1)}, f32[896,128]{1,0:T(8,128)}, u32[]{:S(2)}) copy-start(f32[896,128]{1,0:T(8,128)} %param.8) | copy-start | bytes 1376260
  58.4 91.1 %copy-start.2 = (f32[896,128]{1,0:T(8,128)S(1)}, f32[896,128]{1,0:T(8,128)}, u32[]{:S(2)}) copy-start(f32[896,128]{1,0:T(8,128)} %param.9) | copy-start | bytes 1376260
  58.4 170.5 %copy-start.3 = (bf16[256,128]{1,0:T(8,128)(2,1)S(1)}, bf16[256,128]{1,0:T(8,128)(2,1)}, u32[]{:S(2)}) copy-start(bf16[256,128]{1,0:T(8,128)(2,1)} %param.7) | copy-start | bytes 196612
  58.4 120.1 %all-reduce.2.cloned.1.call-start = ((), (), s32[]{:S(2)}) async-start(), calls=%async_computation.4 | async-start | bytes 917504 | tf_op jit(solution)/shard_map/psum | solution.py:28
  149.2 79.6 %all-gather.5.cloned.1.call-start = ((), (), s32[]{:S(2)}) async-start(), calls=%async_computation.2 | async-start | bytes 3899392 | tf_op jit(solution)/shard_map/all_gather | solution.py:34
Sparse Core Ops, SparseCore 0:
  10.1 40.5 all-gather.2
  58.5 90.6 reduce-scatter.1
  151.5 26.9 all-reduce.1
  181.1 47.7 all-gather.4
where the time goes:
time: 253 us
  waiting for transfers between devices  209 us (83%)
  matrix products  14.7 us (6%)
  between operations  13.8 us (5%)
  local copies, waits for them, and re-layouts  12.5 us (5%)
    reduce_scatter x1, waiting for transfers between devices, local(): low_rank = lax.psum_scatter(whole, 'fsdp', scatter_dimension=0, tiled=True)  90.7 us
    all_gather x1, waiting for transfers between devices, local(): lax.all_gather(normalized, 'fsdp', axis=0, tiled=True)  46.4 us
    all_gather x1, waiting for transfers between devices, local(): lax.all_gather(projection, 'fsdp', axis=0, tiled=True)  42.8 us
    psum x1, waiting for transfers between devices, local(): whole = lax.psum(whole, 'dp')  28.8 us
    unnamed x13, local copies, waits for them, and re-layouts  12.5 us
    dot_general x1, matrix products, local(): lax.dot_general(grad_out, projected, contract, preferred_element_type=jnp...  7.64 us
    dot_general x1, matrix products, local(): lax.dot_general(projection, lax.all_gather(normalized, 'fsdp', axis=0, ti...  7.09 us
  transfers between devices with their start and end apart: 4, of which 4 were waited for; matrix products, arithmetic and copies ran while one was open for 1% of the time, Pallas kernels for 0%

commit v1 on v0

--- a/solution.py
+++ b/solution.py
@@ -25,7 +25,7 @@
     ).astype(jnp.bfloat16)
     contract = (((0,), (0,)), ((), ()))
     whole = lax.dot_general(grad_out, projected, contract, preferred_element_type=jnp.float32)
-    whole = lax.psum(whole, "dp")
+    whole = jnp.sum(lax.all_gather(whole, "dp"), axis=0)
     low_rank = lax.psum_scatter(whole, "fsdp", scatter_dimension=0, tiled=True)
     new_moment, new_second, normalized = adam_step(low_rank, moment, second)
     expand = (((1,), (1,)), ((), ()))

time: 253 us -> 439 us (1.74)
  waiting for transfers between devices: 209 us -> 355 us
  other arithmetic: 2.01 us -> 23.8 us
  local copies, waits for them, and re-layouts: 12.5 us -> 30.8 us
    all_gather x0 -> x1, waiting for transfers between devices: none -> 175 us  [local(): whole = jnp.sum(lax.all_gather(whole, 'dp'), axis=0)]
    psum x1 -> x0, waiting for transfers between devices: 28.8 us -> none  [local(): whole = lax.psum(whole, 'dp')]
    reduce_sum x0 -> x1, other arithmetic: none -> 21.8 us  [local(): whole = jnp.sum(lax.all_gather(whole, 'dp'), axis=0)]
    all_gather x0 -> x1, local copies, waits for them, and re-layouts: none -> 17.4 us  [local(): whole = jnp.sum(lax.all_gather(whole, 'dp'), axis=0)]
    unnamed x13 -> x15, local copies, waits for them, and re-layouts: 12.5 us -> 13.4 us
where the time goes in v1:
time: 439 us; the launch traced here: 438 us
  waiting for transfers between devices  355 us (81%)
  local copies, waits for them, and re-layouts  30.8 us (7%)
  other arithmetic  23.8 us (5%)
  matrix products  14.8 us (3%)
  between operations  13.8 us (3%)
    all_gather x1, waiting for transfers between devices, local(): whole = jnp.sum(lax.all_gather(whole, 'dp'), axis=0)  175 us
    reduce_scatter x1, waiting for transfers between devices, local(): low_rank = lax.psum_scatter(whole, 'fsdp', scatter_dimension=0, tiled=True)  90.4 us
    all_gather x1, waiting for transfers between devices, local(): lax.all_gather(normalized, 'fsdp', axis=0, tiled=True)  46.1 us
    all_gather x1, waiting for transfers between devices, local(): lax.all_gather(projection, 'fsdp', axis=0, tiled=True)  42.8 us
    reduce_sum x1, other arithmetic, local(): whole = jnp.sum(lax.all_gather(whole, 'dp'), axis=0)  21.8 us
    all_gather x1, local copies, waits for them, and re-layouts, local(): whole = jnp.sum(lax.all_gather(whole, 'dp'), axis=0)  17.4 us
    unnamed x15, local copies, waits for them, and re-layouts  13.4 us
  transfers between devices with their start and end apart: 4, of which 4 were waited for; matrix products, arithmetic and copies ran while one was open for 1% of the time, Pallas kernels for 0%

profile of v1, /device:TPU:0, one launch (start us, length us, event | category | flops | bytes accessed | tf_op | source)
XLA Modules:
  0.0 438.0 jit_solution(8605379560197742551)
XLA Ops:
  7.2 0.0 copy-start
  7.2 0.0 all-gather.5.cloned.1.call-start
  7.2 0.7 all-gather.5.cloned.1.call-update
  7.9 0.0 all-gather.9.cloned.1.call-start
  8.0 42.8 %all-gather.5.cloned.1.call-done = bf16[4096,128]{1,0:T(8,128)(2,1)} async-done(((bf16[256,128]{1,0:T(8,128)(2,1)}), bf16[4096,128]{1,0:T(8,128)(2,1)}) %all-gather.5.cloned.1.call-update) | async-done | bytes 1048592 | tf_op jit(solution)/shard_map/all_gather | solution.py:23
  50.7 0.0 copy-done
  50.7 7.6 %convolution_bitcast_fusion = f32[14336,128]{0,1:T(8,128)} fusion(bf16[192,14336]{1,0:T(8,128)(2,1)} %param.6, bf16[192,4096]{1,0:T(8,128)(2,1)S(1)} %copy-done, bf16[4096,128]{1,0:T(8,128)(2,1)} %all-gather.5.cloned.1.call-done), kind=kOutput, calls=%fused_computation.2 | convolution fusion | flops 905994240 | bytes 15466496 | tf_op jit(solution)/shard_map/dot_general | solution.py:27
  58.4 0.0 all-gather.9.cloned.1.call-update
  58.4 0.0 reduce-scatter.2.cloned.1.call-start
  58.5 174.5 %all-gather.9.cloned.1.call-done = f32[28672,128]{0,1:T(8,128)} async-done(((f32[14336,128]{0,1:T(8,128)}), f32[28672,128]{0,1:T(8,128)}) %all-gather.9.cloned.1.call-update) | async-done | bytes 14680080 | tf_op jit(solution)/shard_map/all_gather | solution.py:28
  233.0 17.4 %reshape.6 = f32[2,14336,128]{1,0,2:T(2,128)} reshape(f32[28672,128]{0,1:T(8,128)} %all-gather.9.cloned.1.call-done) | data formatting | bytes 29360128 | tf_op jit(solution)/shard_map/all_gather | solution.py:28
  250.4 21.8 %reduce_sum.9 = f32[14336,128]{0,1:T(8,128)} reduce(f32[2,14336,128]{1,0,2:T(2,128)} %reshape.6, f32[]{:T(128)} %constant.3.clone.1), dimensions={0}, to_apply=%region_0.0 | reduce | flops 1835008 | bytes 22020100 | tf_op jit(solution)/shard_map/reduce_sum | solution.py:28
  272.2 0.0 copy-start.2
  272.2 0.0 copy-start.3
  272.2 0.0 copy-start.4
  272.2 0.0 reduce-scatter.2.cloned.1.call-update
  272.2 0.0 all-gather.7.cloned.1.call-start
  272.3 0.9 copy-done.2
  273.2 0.2 copy.10
  273.4 0.0 copy-done.3
  273.4 0.2 copy.9
  273.6 90.4 %reduce-scatter.2.cloned.1.call-done = f32[896,128]{0,1:T(8,128)} async-done(((f32[14336,128]{0,1:T(8,128)}), f32[896,128]{0,1:T(8,128)}) %reduce-scatter.2.cloned.1.call-update) | async-done | bytes 458768 | tf_op jit(solution)/shard_map/reduce_scatter | solution.py:29
  364.0 2.0 divide_convert_fusion
  366.0 0.0 all-gather.7.cloned.1.call-update
  366.1 1.0 copy.12
  367.0 1.0 copy.13
  368.0 46.1 %all-gather.7.cloned.1.call-done = bf16[14336,128]{0,1:T(8,128)(2,1)} async-done(((bf16[896,128]{0,1:T(8,128)(2,1)}), bf16[14336,128]{0,1:T(8,128)(2,1)}) %all-gather.7.cloned.1.call-update) | async-done | bytes 3670032 | tf_op jit(solution)/shard_map/all_gather | solution.py:34
  414.1 0.0 copy-done.4
  414.1 0.0 copy-start.1
  414.2 7.2 %fusion = bf16[256,14336]{0,1:T(8,128)(2,1)} fusion(bf16[14336,128]{0,1:T(8,128)(2,1)} %all-gather.7.cloned.1.call-done, bf16[256,128]{1,0:T(8,128)(2,1)S(1)} %copy-done.4), kind=kOutput, calls=%fused_computation.1 | convolution fusion | flops 943194112 | bytes 11075584 | tf_op jit(solution)/shard_map/dot_general | solution.py:32
  421.4 10.1 %copy.11 = bf16[256,14336]{1,0:T(8,128)(2,1)} copy(bf16[256,14336]{0,1:T(8,128)(2,1)} %fusion) | data formatting | bytes 14680064
  431.5 0.0 copy-done.1
Async XLA Ops:
  7.2 43.6 %copy-start = (bf16[192,4096]{1,0:T(8,128)(2,1)S(1)}, bf16[192,4096]{1,0:T(8,128)(2,1)}, u32[]{:S(2)}) copy-start(bf16[192,4096]{1,0:T(8,128)(2,1)} %param.5) | copy-start | bytes 4718596
  7.2 43.6 %all-gather.5.cloned.1.call-start = ((), (), s32[]{:S(2)}) async-start(), calls=%async_computation.1 | async-start | bytes 1114112 | tf_op jit(solution)/shard_map/all_gather | solution.py:23
  7.9 225.1 %all-gather.9.cloned.1.call-start = ((), (), s32[]{:S(2)}) async-start(), calls=%async_computation.4 | async-start | bytes 22020096 | tf_op jit(solution)/shard_map/all_gather | solution.py:28
  58.4 305.6 %reduce-scatter.2.cloned.1.call-start = ((), (), s32[]{:S(2)}) async-start(), calls=%async_computation.2 | async-start | bytes 7798784 | tf_op jit(solution)/shard_map/reduce_scatter | solution.py:29
  272.2 1.0 copy-start.2
  272.2 1.2 copy-start.3
  272.2 141.9 %copy-start.4 = (bf16[256,128]{1,0:T(8,128)(2,1)S(1)}, bf16[256,128]{1,0:T(8,128)(2,1)}, u32[]{:S(2)}) copy-start(bf16[256,128]{1,0:T(8,128)(2,1)} %param.7) | copy-start | bytes 196612
  272.2 141.9 %all-gather.7.cloned.1.call-start = ((), (), s32[]{:S(2)}) async-start(), calls=%async_computation.3 | async-start | bytes 3899392 | tf_op jit(solution)/shard_map/all_gather | solution.py:34
  414.1 17.3 %copy-start.1 = (bf16[192,4096]{1,0:T(8,128)(2,1)S(1)}, bf16[192,4096]{1,0:T(8,128)(2,1)}, u32[]{:S(2)}) copy-start(bf16[192,4096]{1,0:T(8,128)(2,1)} %param.5) | copy-start | bytes 4718596
Sparse Core Ops, SparseCore 0:
  10.2 40.5 all-gather.4
  58.5 174.4 all-gather.8
  272.4 91.6 reduce-scatter.1
  366.6 47.4 all-gather.6
